TPU v7x, 256 devices: a whole 4x4x8 slice. The times are simulated.
256 devices in a mesh: depth: 4 (over z_lo, core), scan: 64 (over z_hi, x, y).
Axes of the slice: x: 4, y: 4, z: 8 (z_hi: 4, z_lo: 2; z = z_hi * 2 + z_lo), core: 2. Of those that a mesh axis runs over, the one named last changes fastest.
Arguments:
- probe_wave: bfloat16 [2, 512, 512], replicated, may hold values from -6 to 6
- prop_rows: bfloat16 [2, 512, 512], replicated, may hold values from -0.1875 to 0.1875
- prop_cols: bfloat16 [2, 512, 512], replicated, may hold values from -0.1875 to 0.1875
- transmission: bfloat16 [4, 2, 768, 768], P('depth', None, 'scan'), may hold values from -0.5 to 1.3, as said below
- exit_cotangent: bfloat16 [128, 2, 512, 512], P('scan'), may hold values from -1.1953125 to 1.1953125
- window_tiles: int32 [128, 2], P('scan'), may hold values from 0 to 8
- slot_count: int32 [64], P('scan'), may hold values from 1 to 2, as said below
Outputs:
- object_grad: float32 [4, 2, 768, 768], P('depth', None, 'scan')
Inputs may be any that keep to these rules, and one draw needn't show every extreme that they name: `window_tiles`: a window starts 32 times these indices and stays inside the slice. The first slot_count[j] slots of scan index j are used and the others are ignored; some scan index uses all 2 slots and some uses one. `transmission`: real parts lie in 0.6 to 1.3 and imaginary parts in -0.5 to 0.5.
All inputs are finite; a program needn't handle non-finite values.
Results may differ from a plain program's by a relative error of at most 0.014.
Values may be sent and summed in bfloat16 or wider, within the bound.
No kernel may reach another device: no remote copies, remote signals or barrier semaphores. Data moves between devices by JAX's collectives and lax.ppermute only.
A program may use at most 128 MiB of HBM per device.

v0:
```python
import jax
import jax.numpy as jnp
from jax import lax
from jax.sharding import PartitionSpec as P

TILE = 32


def shifted(value, axis, steps):
    count = lax.axis_size(axis)
    leading, last = (max(0, -steps), min(count, count - steps))
    return lax.ppermute(value, axis, [(source, source + steps) for source in range(leading, last)])


def rows_product(matrix, field):
    real = jnp.dot(matrix[0], field[0], preferred_element_type=jnp.float32) - jnp.dot(
        matrix[1], field[1], preferred_element_type=jnp.float32
    )
    imag = jnp.dot(matrix[0], field[1], preferred_element_type=jnp.float32) + jnp.dot(
        matrix[1], field[0], preferred_element_type=jnp.float32
    )
    return jnp.stack([real, imag])


def right_transpose(left, right):
    return lax.dot_general(
        left, right, (((1,), (1,)), ((), ())), preferred_element_type=jnp.float32
    )


def cols_product(field, matrix):
    real = right_transpose(field[0], matrix[0]) - right_transpose(field[1], matrix[1])
    imag = right_transpose(field[1], matrix[0]) + right_transpose(field[0], matrix[1])
    return jnp.stack([real, imag])


def left_transpose(left, right):
    return lax.dot_general(
        left, right, (((0,), (0,)), ((), ())), preferred_element_type=jnp.float32
    )


def adjoint_rows(matrix, field):
    real = left_transpose(matrix[0], field[0]) + left_transpose(matrix[1], field[1])
    imag = left_transpose(matrix[0], field[1]) - left_transpose(matrix[1], field[0])
    return jnp.stack([real, imag])


def conj_cols(field, matrix):
    real = jnp.dot(field[0], matrix[0], preferred_element_type=jnp.float32) + jnp.dot(
        field[1], matrix[1], preferred_element_type=jnp.float32
    )
    imag = jnp.dot(field[1], matrix[0], preferred_element_type=jnp.float32) - jnp.dot(
        field[0], matrix[1], preferred_element_type=jnp.float32
    )
    return jnp.stack([real, imag])


def complex_times(first, second):
    a0 = first[0].astype(jnp.float32)
    a1 = first[1].astype(jnp.float32)
    b0 = second[0].astype(jnp.float32)
    b1 = second[1].astype(jnp.float32)
    return jnp.stack([a0 * b0 - a1 * b1, a0 * b1 + a1 * b0])


def conj_times(first, second):
    a0 = first[0].astype(jnp.float32)
    a1 = first[1].astype(jnp.float32)
    b0 = second[0]
    b1 = second[1]
    return jnp.stack([a0 * b0 + a1 * b1, a0 * b1 - a1 * b0])


def on_device(
    probe_wave, prop_rows, prop_cols, transmission, exit_cotangent, window_tiles, slot_count
):
    depth_count = lax.axis_size("depth")
    depth_index = lax.axis_index("depth")
    slots = exit_cotangent.shape[0]
    width = probe_wave.shape[-1]
    ticks = slots + depth_count - 1
    used_slots = slot_count[0]
    whole = lax.all_gather(transmission[0], "scan", axis=1, tiled=True)
    zero = jnp.zeros((), jnp.int32)

    def window_start(slot):
        return (window_tiles[slot, 0] * TILE, window_tiles[slot, 1] * TILE)

    def patch_of(slot):
        row_start, col_start = window_start(slot)
        return lax.dynamic_slice(whole, (zero, row_start, col_start), (2, width, width))

    empty_wave = jnp.zeros((2, width, width), jnp.bfloat16)
    stored = jnp.zeros((slots, 2, width, width), jnp.bfloat16)
    incoming = empty_wave
    for tick in range(ticks):
        slot = tick - depth_index
        active = (slot >= 0) & (slot < slots) & (slot < used_slots)
        safe = jnp.clip(slot, 0, slots - 1)
        wave = jnp.where(depth_index == 0, probe_wave, incoming)
        kept = jnp.where(active, wave, stored[safe])
        stored = lax.dynamic_update_index_in_dim(stored, kept, safe, 0)

        def advance():
            product = complex_times(wave, patch_of(safe)).astype(jnp.bfloat16)
            swept = rows_product(prop_rows, product).astype(jnp.bfloat16)
            return cols_product(swept, prop_cols).astype(jnp.bfloat16)

        outgoing = lax.cond(active & (depth_index < depth_count - 1), advance, lambda: empty_wave)
        incoming = shifted(outgoing, "depth", 1)
    grad = jnp.zeros(whole.shape, jnp.float32)
    incoming = empty_wave
    empty_term = jnp.zeros((2, width, width), jnp.float32)
    for tick in range(ticks):
        slot = tick - (depth_count - 1 - depth_index)
        active = (slot >= 0) & (slot < slots) & (slot < used_slots)
        safe = jnp.clip(slot, 0, slots - 1)
        upstream = jnp.where(depth_index == depth_count - 1, exit_cotangent[safe], incoming)

        def retreat():
            swept = adjoint_rows(prop_rows, upstream).astype(jnp.bfloat16)
            adjoint = conj_cols(swept, prop_cols)
            contrib = conj_times(stored[safe], adjoint)
            return (contrib, conj_times(patch_of(safe), adjoint).astype(jnp.bfloat16))

        contrib, outgoing = lax.cond(active, retreat, lambda: (empty_term, empty_wave))
        row_start, col_start = window_start(safe)
        current = lax.dynamic_slice(grad, (zero, row_start, col_start), (2, width, width))
        grad = lax.dynamic_update_slice(grad, current + contrib, (zero, row_start, col_start))
        incoming = shifted(outgoing, "depth", -1)
    total = lax.psum_scatter(grad, "scan", scatter_dimension=1, tiled=True)
    return total[None]


def solution(mesh):
    placed = (
        P(),
        P(),
        P(),
        P("depth", None, "scan", None),
        P("scan", None, None, None),
        P("scan", None),
        P("scan"),
    )
    return jax.shard_map(
        on_device,
        mesh=mesh,
        in_specs=placed,
        out_specs=P("depth", None, "scan", None),
        check_vma=False,
    )
```

profile of v0, /device:TPU:8, one launch (start us, length us, event | category | flops | bytes accessed | tf_op | source)
XLA Modules:
  0.0 1586.8 jit_solution(9367382944052077562)
XLA Ops:
  11.3 81.5 %all-gather.3.cloned.1.call-done = bf16[1,2,768,768]{3,1,0,2:T(2,128)(2,1)} async-done(((bf16[1,2,12,768]{3,1,0,2:T(2,128)(2,1)}), bf16[1,2,768,768]{3,1,0,2:T(2,128)(2,1)}) %all-gather.3.cloned.1.call-update) | async-done | bytes 2359312 | tf_op jit(solution)/shard_map/all_gather | solution.py:84
  92.8 12.7 conditional.9
  92.8 3.4 copy.15
  112.3 16.7 %collective-permute-start.1 = (bf16[2,512,512]{2,1,0:T(8,128)(2,1)}, bf16[2,512,512]{2,1,0:T(8,128)(2,1)}, u32[]{:S(2)}, u32[]{:S(2)}) collective-permute-start(bf16[2,512,512]{2,1,0:T(8,128)(2,1)} %get-tuple-element.591), channel_id=1, source_target_pairs={{0,64},{64,128},{128,192},{1,65},{65,129},{129,193},{2,66},{66,130... | collective-permute-start | bytes 3145736 | tf_op jit(solution)/shard_map/ppermute | solution.py:12
  133.2 13.4 collective-permute-start.2
  151.1 27.8 %collective-permute-start.3 = (bf16[2,512,512]{2,1,0:T(8,128)(2,1)}, bf16[2,512,512]{2,1,0:T(8,128)(2,1)}, u32[]{:S(2)}, u32[]{:S(2)}) collective-permute-start(bf16[2,512,512]{2,1,0:T(8,128)(2,1)} %get-tuple-element.593), channel_id=1, source_target_pairs={{0,64},{64,128},{128,192},{1,65},{65,129},{129,193},{2,66},{66,130... | collective-permute-start | bytes 3145736 | tf_op jit(solution)/shard_map/ppermute | solution.py:12
  186.4 16.1 %collective-permute-done.4 = bf16[2,512,512]{2,1,0:T(8,128)(2,1)S(1)} collective-permute-done((bf16[2,512,512]{2,1,0:T(8,128)(2,1)}, bf16[2,512,512]{2,1,0:T(8,128)(2,1)S(1)}, u32[]{:S(2)}, u32[]{:S(2)}) %collective-permute-start.4) | collective-permute-done | bytes 1048608 | tf_op jit(solution)/shard_map/ppermute | solution.py:12
  202.5 3.1 conditional.14
  206.9 15.8 collective-permute-done.5
  222.7 3.2 conditional.15
  227.2 44.8 %collective-permute-done.6 = bf16[2,512,512]{2,1,0:T(8,128)(2,1)S(1)} collective-permute-done((bf16[2,512,512]{2,1,0:T(8,128)(2,1)}, bf16[2,512,512]{2,1,0:T(8,128)(2,1)S(1)}, u32[]{:S(2)}, u32[]{:S(2)}) %collective-permute-start.6) | collective-permute-done | bytes 1048608 | tf_op jit(solution)/shard_map/ppermute | solution.py:12
  272.0 19.2 %conditional.16 = (bf16[2,512,512]{2,1,0:T(8,128)(2,1)}, f32[2,512,512]{2,0,1:T(2,128)}) conditional(s32[]{:T(128)} %convert_element_type.243, () %tuple.81, (s32[]{:T(128)}, bf16[2,2,512,512]{3,2,1,0:T(8,128)(2,1)}, bf16[2,512,512]{2,1,0:T(8,128)(2,1)S(1)}, pred[]{:T(512)}, bf16[2,512,512]{2,1,0:T(8,128)(2,1)S(1)}, ...), branch_computations={%region_14.15_spmd, %region_15.16_spmd.clone.clone} | conditional | flops 2155347968 | bytes 47710424 | solution.py:127
  277.6 3.4 copy.44
  299.8 3.4 broadcast_in_dim.40
  303.2 95.6 %dynamic_update_slice.36 = f32[2,768,768]{2,0,1:T(2,128)} dynamic-update-slice(f32[2,768,768]{2,0,1:T(2,128)} %broadcast_in_dim.40, f32[2,512,512]{2,0,1:T(2,128)} %get-tuple-element.413, s32[]{:T(128)} %constant.173.clone.1, s32[]{:T(128)S(6)} %select_n.250, s32[]{:T(128)S(6)} %select_n.251) | dynamic-update-slice | bytes 4194308 | tf_op jit(solution)/shard_map/dynamic_update_slice | solution.py:130
  398.8 5.9 dynamic-slice_add_fusion.3
  404.7 95.6 %dynamic_update_slice.37 = f32[2,768,768]{2,0,1:T(2,128)} dynamic-update-slice(f32[2,768,768]{2,0,1:T(2,128)} %dynamic_update_slice.36, f32[2,512,512]{2,0,1:T(2,128)} %dynamic-slice_add_fusion.3, s32[]{:T(128)} %constant.173.clone.1, s32[]{:T(128)S(6)} %select_n.252, s32[]{:T(128)S(6)} %select_n.253) | dynamic-update-slice | bytes 4194308 | tf_op jit(solution)/shard_map/dynamic_update_slice | solution.py:130
  500.3 5.9 dynamic-slice_add_fusion.2
  506.2 95.6 %dynamic_update_slice.38 = f32[2,768,768]{2,0,1:T(2,128)} dynamic-update-slice(f32[2,768,768]{2,0,1:T(2,128)} %dynamic_update_slice.37, f32[2,512,512]{2,0,1:T(2,128)} %dynamic-slice_add_fusion.2, s32[]{:T(128)} %constant.173.clone.1, s32[]{:T(128)S(6)} %select_n.256, s32[]{:T(128)S(6)} %select_n.257) | dynamic-update-slice | bytes 4194308 | tf_op jit(solution)/shard_map/dynamic_update_slice | solution.py:130
  601.8 5.9 dynamic-slice_add_fusion.1
  607.7 95.6 %dynamic_update_slice.39 = f32[2,768,768]{2,0,1:T(2,128)} dynamic-update-slice(f32[2,768,768]{2,0,1:T(2,128)} %dynamic_update_slice.38, f32[2,512,512]{2,0,1:T(2,128)} %dynamic-slice_add_fusion.1, s32[]{:T(128)} %constant.173.clone.1, s32[]{:T(128)S(6)} %select_n.259, s32[]{:T(128)S(6)} %select_n.260) | dynamic-update-slice | bytes 4194308 | tf_op jit(solution)/shard_map/dynamic_update_slice | solution.py:130
  705.4 4.6 dynamic-slice_add_fusion
  710.0 39.7 %dynamic_update_slice.40 = f32[2,768,768]{2,0,1:T(2,128)} dynamic-update-slice(f32[2,768,768]{2,0,1:T(2,128)} %dynamic_update_slice.39, f32[2,512,512]{2,0,1:T(2,128)S(1)} %dynamic-slice_add_fusion, s32[]{:T(128)} %constant.173.clone.1, s32[]{:T(128)S(6)} %select_n.262, s32[]{:T(128)S(6)} %select_n.263) | dynamic-update-slice | bytes 4194308 | tf_op jit(solution)/shard_map/dynamic_update_slice | solution.py:130
  751.6 826.7 %all-reduce.3.cloned.1.call-done = f32[2,768,768]{2,0,1:T(2,128)} async-done(((f32[2,768,768]{2,0,1:T(2,128)}), f32[2,768,768]{2,0,1:T(2,128)}) %all-reduce.3.cloned.1.call-update) | async-done | bytes 4718608
  (82 shorter events, 71.2 us)
Async XLA Ops:
  6.5 3.0 copy-start.2
  6.5 86.3 %all-gather.3.cloned.1.call-start = ((), (), s32[]{:S(2)}) async-start(), calls=%async_computation | async-start | bytes 2396160 | tf_op jit(solution)/shard_map/all_gather | solution.py:84
  7.3 1571.0 %all-reduce.3.cloned.1.call-start = ((), (), s32[]{:S(2)}) async-start(), calls=%async_computation.1 | async-start | bytes 9437184
  9.5 83.3 %copy-start = (bf16[2,512,512]{2,1,0:T(8,128)(2,1)S(1)}, bf16[2,512,512]{2,1,0:T(8,128)(2,1)}, u32[]{:S(2)}) copy-start(bf16[2,512,512]{2,1,0:T(8,128)(2,1)} %param.27) | copy-start | bytes 3145732
  9.5 83.3 %copy-start.1 = (bf16[2,512,512]{2,1,0:T(8,128)(2,1)S(1)}, bf16[2,512,512]{2,1,0:T(8,128)(2,1)}, u32[]{:S(2)}) copy-start(bf16[2,512,512]{2,1,0:T(8,128)(2,1)} %param.26) | copy-start | bytes 3145732
  9.5 83.3 %copy-start.9 = (s32[2,2]{1,0:T(2,128)S(1)}, s32[2,2]{1,0:T(2,128)}, u32[]{:S(2)}) copy-start(s32[2,2]{1,0:T(2,128)} %param.30) | copy-start | bytes 52
  105.5 3.9 collective-permute-start
  112.3 18.0 %collective-permute-start.1 = (bf16[2,512,512]{2,1,0:T(8,128)(2,1)}, bf16[2,512,512]{2,1,0:T(8,128)(2,1)}, u32[]{:S(2)}, u32[]{:S(2)}) collective-permute-start(bf16[2,512,512]{2,1,0:T(8,128)(2,1)} %get-tuple-element.591), channel_id=1, source_target_pairs={{0,64},{64,128},{128,192},{1,65},{65,129},{129,193},{2,66},{66,130... | collective-permute-start | bytes 3145736 | tf_op jit(solution)/shard_map/ppermute | solution.py:12
  133.2 15.0 collective-permute-start.2
  151.1 29.5 %collective-permute-start.3 = (bf16[2,512,512]{2,1,0:T(8,128)(2,1)}, bf16[2,512,512]{2,1,0:T(8,128)(2,1)}, u32[]{:S(2)}, u32[]{:S(2)}) collective-permute-start(bf16[2,512,512]{2,1,0:T(8,128)(2,1)} %get-tuple-element.593), channel_id=1, source_target_pairs={{0,64},{64,128},{128,192},{1,65},{65,129},{129,193},{2,66},{66,130... | collective-permute-start | bytes 3145736 | tf_op jit(solution)/shard_map/ppermute | solution.py:12
  180.2 1.8 copy-start.3
  185.1 17.4 %collective-permute-start.4 = (bf16[2,512,512]{2,1,0:T(8,128)(2,1)}, bf16[2,512,512]{2,1,0:T(8,128)(2,1)S(1)}, u32[]{:S(2)}, u32[]{:S(2)}) collective-permute-start(bf16[2,512,512]{2,1,0:T(8,128)(2,1)} %get-tuple-element.200), channel_id=1, source_target_pairs={{64,0},{128,64},{192,128},{65,1},{129,65},{193,129},{66,2},{130,66... | collective-permute-start | bytes 3145736 | tf_op jit(solution)/shard_map/ppermute | solution.py:12
  205.6 17.1 %collective-permute-start.5 = (bf16[2,512,512]{2,1,0:T(8,128)(2,1)}, bf16[2,512,512]{2,1,0:T(8,128)(2,1)S(1)}, u32[]{:S(2)}, u32[]{:S(2)}) collective-permute-start(bf16[2,512,512]{2,1,0:T(8,128)(2,1)} %get-tuple-element.202), channel_id=1, source_target_pairs={{64,0},{128,64},{192,128},{65,1},{129,65},{193,129},{66,2},{130,66... | collective-permute-start | bytes 3145736 | tf_op jit(solution)/shard_map/ppermute | solution.py:12
  225.9 46.1 %collective-permute-start.6 = (bf16[2,512,512]{2,1,0:T(8,128)(2,1)}, bf16[2,512,512]{2,1,0:T(8,128)(2,1)S(1)}, u32[]{:S(2)}, u32[]{:S(2)}) collective-permute-start(bf16[2,512,512]{2,1,0:T(8,128)(2,1)} %get-tuple-element.204), channel_id=1, source_target_pairs={{64,0},{128,64},{192,128},{65,1},{129,65},{193,129},{66,2},{130,66... | collective-permute-start | bytes 3145736 | tf_op jit(solution)/shard_map/ppermute | solution.py:12
  282.9 1.2 copy-start.8
  291.3 412.0 %collective-permute-start.7 = (bf16[2,512,512]{2,1,0:T(8,128)(2,1)}, bf16[2,512,512]{2,1,0:T(8,128)(2,1)S(1)}, u32[]{:S(2)}, u32[]{:S(2)}) collective-permute-start(bf16[2,512,512]{2,1,0:T(8,128)(2,1)} %get-tuple-element.206), channel_id=1, source_target_pairs={{64,0},{128,64},{192,128},{65,1},{129,65},{193,129},{66,2},{130,66... | collective-permute-start | bytes 3145736 | tf_op jit(solution)/shard_map/ppermute | solution.py:12
  704.0 1.3 copy-start.4
  749.7 0.7 copy-start.10
Sparse Core Ops, SparseCore 0:
  10.5 82.2 all-gather.2
  749.8 828.3 all-reduce.2
where the time goes:
time: 1610 us; the launch traced here: 1590 us
  waiting for transfers between devices  986 us (61%)
  local copies, waits for them, and re-layouts  461 us (29%)
  starting transfers between devices  65.5 us (4%)
  other arithmetic  37.2 us (2%)
  between operations  21.5 us (1%)
    unnamed x3, waiting for transfers between devices  827 us
    dynamic_update_slice x5, local copies, waits for them, and re-layouts, on_device(): lax.dynamic_update_slice(grad, current + contrib, (zero, row_start, col_s...  422 us
    all_gather x1, waiting for transfers between devices, on_device(): whole = lax.all_gather(transmission[0], 'scan', axis=1, tiled=True)  81.5 us
    ppermute x8, waiting for transfers between devices, shifted(): lax.ppermute(value, axis, [(source, source + steps) for source in range(l...  77.6 us
    ppermute x8, starting transfers between devices, shifted(): lax.ppermute(value, axis, [(source, source + steps) for source in range(l...  65.5 us
  transfers between devices with their start and end apart: 10, of which 8 were waited for; matrix products, arithmetic and copies ran while one was open for 26% of the time, Pallas kernels for 0%

commit v1 on v0

--- a/solution.py
+++ b/solution.py
@@ -81,7 +81,9 @@
     width = probe_wave.shape[-1]
     ticks = slots + depth_count - 1
     used_slots = slot_count[0]
-    whole = lax.all_gather(transmission[0], "scan", axis=1, tiled=True)
+    whole = jnp.concatenate(
+        lax.all_to_all(jnp.stack([transmission[0]] * lax.axis_size("scan")), "scan", 0, 0), axis=1
+    )
     zero = jnp.zeros((), jnp.int32)
 
     def window_start(slot):

time: 1610 us -> 1590 us (0.988)
  waiting for transfers between devices: 986 us -> 950 us
    all_gather x1 -> x0, waiting for transfers between devices: 81.5 us -> none  [on_device(): whole = lax.all_gather(transmission[0], 'scan', axis=1, tiled=True)]
    all_to_all x0 -> x1, waiting for transfers between devices: none -> 50.4 us  [on_device(): lax.all_to_all(jnp.stack([transmission[0]] * lax.axis_size('scan')), 'sca...]
    unnamed x3 -> x2, waiting for transfers between devices: 827 us -> 822 us
  transfers between devices with their start and end apart: 10 -> 10, of which waited for: 8 -> 9; matrix products, arithmetic and copies ran while one was open for 26% -> 26% of each run, Pallas kernels for 0% -> 0%
where the time goes in v1:
time: 1590 us; the launch traced here: 1570 us
  waiting for transfers between devices  950 us (60%)
  local copies, waits for them, and re-layouts  463 us (29%)
  starting transfers between devices  80 us (5%)
  other arithmetic  36.2 us (2%)
  between operations  21.3 us (1%)
    unnamed x2, waiting for transfers between devices  822 us
    dynamic_update_slice x5, local copies, waits for them, and re-layouts, on_device(): lax.dynamic_update_slice(grad, current + contrib, (zero, row_start, col_s...  424 us
    ppermute x8, waiting for transfers between devices, shifted(): lax.ppermute(value, axis, [(source, source + steps) for source in range(l...  77.3 us
    ppermute x8, starting transfers between devices, shifted(): lax.ppermute(value, axis, [(source, source + steps) for source in range(l...  65.4 us
    all_to_all x1, waiting for transfers between devices, on_device(): lax.all_to_all(jnp.stack([transmission[0]] * lax.axis_size('scan')), 'sca...  50.4 us
  transfers between devices with their start and end apart: 10, of which 9 were waited for; matrix products, arithmetic and copies ran while one was open for 26% of the time, Pallas kernels for 0%

profile of v1, /device:TPU:8, one launch (start us, length us, event | category | flops | bytes accessed | tf_op | source)
XLA Modules:
  0.0 1567.0 jit_solution(17183708722561211244)
XLA Ops:
  6.5 3.4 stack.214
  9.9 14.6 all-to-all-start
  29.6 50.4 %all-to-all-done = bf16[64,2,12,768]{3,1,2,0:T(2,128)(2,1)S(1)} async-done(((bf16[64,2,12,768]{3,1,2,0:T(2,128)(2,1)}), bf16[64,2,12,768]{3,1,2,0:T(2,128)(2,1)S(1)}, u32[]{:S(2)}, u32[]{:S(2)}) %all-to-all-start) | async-done | bytes 2359328 | tf_op jit(solution)/shard_map/all_to_all | solution.py:85
  80.0 11.2 conditional.9
  98.4 18.1 %collective-permute-start.1 = (bf16[2,512,512]{2,1,0:T(8,128)(2,1)}, bf16[2,512,512]{2,1,0:T(8,128)(2,1)}, u32[]{:S(2)}, u32[]{:S(2)}) collective-permute-start(bf16[2,512,512]{2,1,0:T(8,128)(2,1)} %get-tuple-element.655), channel_id=1, source_target_pairs={{0,64},{64,128},{128,192},{1,65},{65,129},{129,193},{2,66},{66,130... | collective-permute-start | bytes 3145736 | tf_op jit(solution)/shard_map/ppermute | solution.py:12
  121.0 13.5 collective-permute-start.2
  139.2 26.1 %collective-permute-start.3 = (bf16[2,512,512]{2,1,0:T(8,128)(2,1)}, bf16[2,512,512]{2,1,0:T(8,128)(2,1)}, u32[]{:S(2)}, u32[]{:S(2)}) collective-permute-start(bf16[2,512,512]{2,1,0:T(8,128)(2,1)} %get-tuple-element.657), channel_id=1, source_target_pairs={{0,64},{64,128},{128,192},{1,65},{65,129},{129,193},{2,66},{66,130... | collective-permute-start | bytes 3145736 | tf_op jit(solution)/shard_map/ppermute | solution.py:12
  173.3 15.5 collective-permute-done.4
  188.9 3.1 conditional.14
  193.3 15.9 %collective-permute-done.5 = bf16[2,512,512]{2,1,0:T(8,128)(2,1)} collective-permute-done((bf16[2,512,512]{2,1,0:T(8,128)(2,1)}, bf16[2,512,512]{2,1,0:T(8,128)(2,1)}, u32[]{:S(2)}, u32[]{:S(2)}) %collective-permute-start.5) | collective-permute-done | bytes 1048608 | tf_op jit(solution)/shard_map/ppermute | solution.py:12
  209.2 3.2 conditional.15
  213.7 45.0 %collective-permute-done.6 = bf16[2,512,512]{2,1,0:T(8,128)(2,1)} collective-permute-done((bf16[2,512,512]{2,1,0:T(8,128)(2,1)}, bf16[2,512,512]{2,1,0:T(8,128)(2,1)}, u32[]{:S(2)}, u32[]{:S(2)}) %collective-permute-start.6) | collective-permute-done | bytes 1048608 | tf_op jit(solution)/shard_map/ppermute | solution.py:12
  258.7 17.7 %conditional.16 = (bf16[2,512,512]{2,1,0:T(8,128)(2,1)}, f32[2,512,512]{2,0,1:T(2,128)S(1)}) conditional(s32[]{:T(128)} %convert_element_type.243, () %tuple.81, (s32[]{:T(128)}, bf16[2,2,512,512]{3,2,1,0:T(8,128)(2,1)}, bf16[2,512,512]{2,1,0:T(8,128)(2,1)}, pred[]{:T(512)}, bf16[2,512,512]{2,1,0:T(8,128)(2,1)S(1)}, ...), branch_computations={%region_14.15_spmd, %region_15.16_spmd.clone.clone} | conditional | flops 2155347968 | bytes 58196296 | solution.py:129
  284.8 3.3 broadcast_in_dim.40
  288.1 95.6 %dynamic_update_slice.36 = f32[2,768,768]{2,0,1:T(2,128)} dynamic-update-slice(f32[2,768,768]{2,0,1:T(2,128)} %broadcast_in_dim.40, f32[2,512,512]{2,0,1:T(2,128)} %get-tuple-element.477, s32[]{:T(128)} %constant.173.clone.1, s32[]{:T(128)S(6)} %select_n.250, s32[]{:T(128)S(6)} %select_n.251) | dynamic-update-slice | bytes 4194308 | tf_op jit(solution)/shard_map/dynamic_update_slice | solution.py:132
  383.7 4.6 dynamic-slice_add_fusion.3
  388.3 96.7 %dynamic_update_slice.37 = f32[2,768,768]{2,0,1:T(2,128)} dynamic-update-slice(f32[2,768,768]{2,0,1:T(2,128)} %dynamic_update_slice.36, f32[2,512,512]{2,0,1:T(2,128)S(1)} %dynamic-slice_add_fusion.3, s32[]{:T(128)} %constant.173.clone.1, s32[]{:T(128)S(6)} %select_n.252, s32[]{:T(128)S(6)} %select_n.253) | dynamic-update-slice | bytes 4194308 | tf_op jit(solution)/shard_map/dynamic_update_slice | solution.py:132
  485.0 4.6 dynamic-slice_add_fusion.2
  489.6 96.7 %dynamic_update_slice.38 = f32[2,768,768]{2,0,1:T(2,128)} dynamic-update-slice(f32[2,768,768]{2,0,1:T(2,128)} %dynamic_update_slice.37, f32[2,512,512]{2,0,1:T(2,128)S(1)} %dynamic-slice_add_fusion.2, s32[]{:T(128)} %constant.173.clone.1, s32[]{:T(128)S(6)} %select_n.256, s32[]{:T(128)S(6)} %select_n.257) | dynamic-update-slice | bytes 4194308 | tf_op jit(solution)/shard_map/dynamic_update_slice | solution.py:132
  586.3 6.0 dynamic-slice_add_fusion.1
  592.2 95.7 %dynamic_update_slice.39 = f32[2,768,768]{2,0,1:T(2,128)} dynamic-update-slice(f32[2,768,768]{2,0,1:T(2,128)} %dynamic_update_slice.38, f32[2,512,512]{2,0,1:T(2,128)} %dynamic-slice_add_fusion.1, s32[]{:T(128)} %constant.173.clone.1, s32[]{:T(128)S(6)} %select_n.259, s32[]{:T(128)S(6)} %select_n.260) | dynamic-update-slice | bytes 4194308 | tf_op jit(solution)/shard_map/dynamic_update_slice | solution.py:132
  690.0 4.6 dynamic-slice_add_fusion
  694.6 39.7 %dynamic_update_slice.40 = f32[2,768,768]{2,0,1:T(2,128)} dynamic-update-slice(f32[2,768,768]{2,0,1:T(2,128)} %dynamic_update_slice.39, f32[2,512,512]{2,0,1:T(2,128)S(1)} %dynamic-slice_add_fusion, s32[]{:T(128)} %constant.173.clone.1, s32[]{:T(128)S(6)} %select_n.262, s32[]{:T(128)S(6)} %select_n.263) | dynamic-update-slice | bytes 4194308 | tf_op jit(solution)/shard_map/dynamic_update_slice | solution.py:132
  736.2 822.1 %all-reduce.3.cloned.1.call-done = f32[2,768,768]{2,0,1:T(2,128)} async-done(((f32[2,768,768]{2,0,1:T(2,128)}), f32[2,768,768]{2,0,1:T(2,128)}) %all-reduce.3.cloned.1.call-update) | async-done | bytes 4718608
  (102 shorter events, 76.7 us)
Async XLA Ops:
  9.9 70.1 %all-to-all-start = ((bf16[64,2,12,768]{3,1,2,0:T(2,128)(2,1)}), bf16[64,2,12,768]{3,1,2,0:T(2,128)(2,1)S(1)}, u32[]{:S(2)}, u32[]{:S(2)}) async-start(bf16[64,2,12,768]{3,1,2,0:T(2,128)(2,1)} %stack.214), calls=%async_computation | async-start | bytes 4718592 | tf_op jit(solution)/shard_map/all_to_all | solution.py:85
  24.5 1533.9 %all-reduce.3.cloned.1.call-start = ((), (), s32[]{:S(2)}) async-start(), calls=%async_computation.1 | async-start | bytes 9437184
  26.7 53.4 %copy-start = (bf16[2,512,512]{2,1,0:T(8,128)(2,1)S(1)}, bf16[2,512,512]{2,1,0:T(8,128)(2,1)}, u32[]{:S(2)}) copy-start(bf16[2,512,512]{2,1,0:T(8,128)(2,1)} %param.27) | copy-start | bytes 3145732
  26.7 53.4 %copy-start.33 = (s32[2,2]{1,0:T(2,128)S(1)}, s32[2,2]{1,0:T(2,128)}, u32[]{:S(2)}) copy-start(s32[2,2]{1,0:T(2,128)} %param.30) | copy-start | bytes 52
  83.7 2.5 copy-start.3
  91.2 3.9 collective-permute-start
  93.5 1.6 copy-start.10
  98.4 19.7 %collective-permute-start.1 = (bf16[2,512,512]{2,1,0:T(8,128)(2,1)}, bf16[2,512,512]{2,1,0:T(8,128)(2,1)}, u32[]{:S(2)}, u32[]{:S(2)}) collective-permute-start(bf16[2,512,512]{2,1,0:T(8,128)(2,1)} %get-tuple-element.655), channel_id=1, source_target_pairs={{0,64},{64,128},{128,192},{1,65},{65,129},{129,193},{2,66},{66,130... | collective-permute-start | bytes 3145736 | tf_op jit(solution)/shard_map/ppermute | solution.py:12
  116.5 1.6 copy-start.11
  121.0 15.2 collective-permute-start.2
  134.6 1.6 copy-start.12
  139.2 27.8 %collective-permute-start.3 = (bf16[2,512,512]{2,1,0:T(8,128)(2,1)}, bf16[2,512,512]{2,1,0:T(8,128)(2,1)}, u32[]{:S(2)}, u32[]{:S(2)}) collective-permute-start(bf16[2,512,512]{2,1,0:T(8,128)(2,1)} %get-tuple-element.657), channel_id=1, source_target_pairs={{0,64},{64,128},{128,192},{1,65},{65,129},{129,193},{2,66},{66,130... | collective-permute-start | bytes 3145736 | tf_op jit(solution)/shard_map/ppermute | solution.py:12
  165.4 1.6 copy-start.13
  166.8 1.7 copy-start.1
  166.8 2.3 copy-start.14
  172.0 16.8 %collective-permute-start.4 = (bf16[2,512,512]{2,1,0:T(8,128)(2,1)}, bf16[2,512,512]{2,1,0:T(8,128)(2,1)}, u32[]{:S(2)}, u32[]{:S(2)}) collective-permute-start(bf16[2,512,512]{2,1,0:T(8,128)(2,1)} %get-tuple-element.200), channel_id=1, source_target_pairs={{64,0},{128,64},{192,128},{65,1},{129,65},{193,129},{66,2},{130,66... | collective-permute-start | bytes 3145736 | tf_op jit(solution)/shard_map/ppermute | solution.py:12
  192.0 17.2 %collective-permute-start.5 = (bf16[2,512,512]{2,1,0:T(8,128)(2,1)}, bf16[2,512,512]{2,1,0:T(8,128)(2,1)}, u32[]{:S(2)}, u32[]{:S(2)}) collective-permute-start(bf16[2,512,512]{2,1,0:T(8,128)(2,1)} %get-tuple-element.202), channel_id=1, source_target_pairs={{64,0},{128,64},{192,128},{65,1},{129,65},{193,129},{66,2},{130,66... | collective-permute-start | bytes 3145736 | tf_op jit(solution)/shard_map/ppermute | solution.py:12
  212.4 46.3 %collective-permute-start.6 = (bf16[2,512,512]{2,1,0:T(8,128)(2,1)}, bf16[2,512,512]{2,1,0:T(8,128)(2,1)}, u32[]{:S(2)}, u32[]{:S(2)}) collective-permute-start(bf16[2,512,512]{2,1,0:T(8,128)(2,1)} %get-tuple-element.204), channel_id=1, source_target_pairs={{64,0},{128,64},{192,128},{65,1},{129,65},{193,129},{66,2},{130,66... | collective-permute-start | bytes 3145736 | tf_op jit(solution)/shard_map/ppermute | solution.py:12
  259.2 1.9 copy-start.9
  267.4 3.3 copy-start.24
  267.4 3.3 copy-start.32
  276.4 11.7 copy-start.15
  276.4 411.4 %collective-permute-start.7 = (bf16[2,512,512]{2,1,0:T(8,128)(2,1)}, bf16[2,512,512]{2,1,0:T(8,128)(2,1)}, u32[]{:S(2)}, u32[]{:S(2)}) collective-permute-start(bf16[2,512,512]{2,1,0:T(8,128)(2,1)} %get-tuple-element.206), channel_id=1, source_target_pairs={{64,0},{128,64},{192,128},{65,1},{129,65},{193,129},{66,2},{130,66... | collective-permute-start | bytes 3145736 | tf_op jit(solution)/shard_map/ppermute | solution.py:12
  592.2 95.7 %copy-start.2 = (bf16[2,512,512]{2,1,0:T(8,128)(2,1)S(1)}, bf16[2,512,512]{2,1,0:T(8,128)(2,1)}, u32[]{:S(2)}) copy-start(bf16[2,512,512]{2,1,0:T(8,128)(2,1)} %param.26) | copy-start | bytes 3145732
  (4 other events, 3.7 us)
Sparse Core Ops, SparseCore 0:
  734.5 823.8 all-reduce.2
